TPU v7x, 256 devices: a whole 4x4x8 slice. The times are simulated.
256 devices in a mesh: tm: 32 (over x, z), tensor: 8 (over y, core).
Axes of the slice: x: 4, y: 4, z: 8, core: 2. Of those that a mesh axis runs over, the one named last changes fastest.
Arguments:
- latents: float32 [32, 640, 64], P('tm', 'tensor'), may hold values from -6 to 6
- residual: bfloat16 [32, 640, 5120], P('tm'), may hold values from -6 to 6
- timesteps: int32 [32], P('tm'), may hold values from 0 to 999
- step_sizes: float32 [32], P('tm'), may hold values from 0.015 to 0.06
- embed_weight: bfloat16 [64, 5120], replicated
- mod_weight: bfloat16 [3, 256, 5120], P(None, None, 'tensor'), may hold values from -0.75 to 0.75
- up_weight: bfloat16 [5120, 7168], P('tm', 'tensor'), may hold values from -0.078125 to 0.078125
- down_weight: bfloat16 [7168, 5120], P('tensor', 'tm'), may hold values from -0.0625 to 0.0625
- head_weight: bfloat16 [5120, 64], replicated, may hold values from -0.078125 to 0.078125
Outputs:
- drift: float32 [32, 640, 64], P('tm', 'tensor')
- new_latents: float32 [32, 640, 64], P('tm', 'tensor')
All inputs are finite; a program needn't handle non-finite values.
Results may differ from a plain program's by a relative error of at most 0.0085.
Values may be sent and summed in bfloat16 or wider, within the bound.
No kernel may reach another device: no remote copies, remote signals or barrier semaphores. Data moves between devices by JAX's collectives and lax.ppermute only.
A program may use at most 128 MiB of HBM per device.

v0:
```python
import math
import jax
import jax.numpy as jnp
from jax import lax
from jax.sharding import PartitionSpec as P


def prefix(part, axis, combine, identity):
    place = lax.axis_index(axis)
    gathered = lax.all_gather(part, axis)
    state = jnp.zeros_like(part) + jnp.asarray(identity, part.dtype)

    def one(hop, state):
        return combine(state, lax.dynamic_index_in_dim(gathered, hop, 0, False))

    return lax.fori_loop(0, place, one, state)


def normalize(values):
    centre = values - jnp.mean(values, axis=-1, keepdims=True)
    spread = jnp.mean(centre * centre, axis=-1, keepdims=True)
    return centre * lax.rsqrt(spread + 1e-06)


def time_features(stamps, width):
    half = width // 2
    freqs = jnp.exp(-math.log(10000.0) * jnp.arange(half, dtype=jnp.float32) / half)
    angles = stamps.astype(jnp.float32)[:, None] * freqs[None, :]
    return jnp.concatenate([jnp.cos(angles), jnp.sin(angles)], axis=-1)


def add_terms(earlier, later):
    return earlier + later


def local(
    latents,
    residual,
    timesteps,
    step_sizes,
    embed_weight,
    mod_weight,
    up_weight,
    down_weight,
    head_weight,
):
    feature = jax.nn.silu(time_features(timesteps, mod_weight.shape[1])).astype(jnp.bfloat16)[0]
    piece_mod = jnp.einsum("f,kfd->kd", feature, mod_weight, preferred_element_type=jnp.float32)
    modulation = lax.all_gather(piece_mod, "tensor", axis=1, tiled=True)
    latent = latents[0]
    stream = residual[0]
    latent_bf = latent.astype(jnp.bfloat16)
    own_rows = latent.shape[0]
    row_start = lax.axis_index("tensor") * own_rows
    own_stream = lax.dynamic_slice_in_dim(stream, row_start, own_rows, 0)
    hidden = own_stream.astype(jnp.float32) + jnp.dot(
        latent_bf, embed_weight, preferred_element_type=jnp.float32
    )
    local_normed = (normalize(hidden) * (1.0 + modulation[1]) + modulation[0]).astype(jnp.bfloat16)
    normed = lax.all_gather(local_normed, "tensor", axis=0, tiled=True)
    preact = jnp.dot(
        normed,
        lax.all_gather(up_weight, "tm", axis=0, tiled=True),
        preferred_element_type=jnp.float32,
    )
    activated = jax.nn.gelu(preact, approximate=True).astype(jnp.bfloat16)
    partial_sums = jnp.dot(
        activated,
        lax.all_gather(down_weight, "tm", axis=1, tiled=True),
        preferred_element_type=jnp.float32,
    )
    mixed = lax.psum_scatter(
        partial_sums.astype(jnp.bfloat16), "tensor", scatter_dimension=0, tiled=True
    ).astype(jnp.float32)
    updated = hidden + modulation[2] * mixed
    drift = jnp.dot(
        normalize(updated).astype(jnp.bfloat16), head_weight, preferred_element_type=jnp.float32
    )
    position = lax.axis_index("tm")
    first = (position == 0).astype(jnp.float32)
    term = first * latent - step_sizes[0] * drift
    earlier = prefix(term, "tm", add_terms, jnp.zeros_like(term))
    new_latent = earlier + term
    return (drift[None], new_latent[None])


def solution(mesh):
    in_specs = (
        P("tm", "tensor", None),
        P("tm", None, None),
        P("tm"),
        P("tm"),
        P(),
        P(None, None, "tensor"),
        P("tm", "tensor"),
        P("tensor", "tm"),
        P(),
    )
    out_specs = (P("tm", "tensor", None), P("tm", "tensor", None))
    return jax.shard_map(local, mesh=mesh, in_specs=in_specs, out_specs=out_specs, check_vma=False)
```

profile of v0, /device:TPU:6, one launch (start us, length us, event | category | flops | bytes accessed | tf_op | source)
XLA Modules:
  0.0 398.8 jit_solution(11767064728763271483)
XLA Ops:
  7.2 1.9 fusion.28
  9.2 0.3 multiply_reduce_fusion.1
  10.3 0.2 fusion.29
  10.5 13.3 %all_gather.18 = f32[3,5120]{1,0:T(4,128)S(1)} all-gather(f32[3,640]{1,0:T(4,128)S(1)} %bitcast.46), channel_id=1, replica_groups=mesh['tm'=32,'tensor'=8] {'tensor'}, dimensions={1}, use_global_device_ids=true | all-gather | bytes 69120 | tf_op jit(solution)/shard_map/all_gather | solution.py:49
  23.9 1.3 add_convert_fusion
  25.2 0.7 all-gather.8.cloned.1.call-update
  26.0 0.7 all-gather.10.cloned.1.call-update
  26.7 45.4 %all-gather.6.cloned.1.call-done = bf16[640,5120]{1,0:T(8,128)(2,1)} async-done(((bf16[80,5120]{1,0:T(8,128)(2,1)}), bf16[640,5120]{1,0:T(8,128)(2,1)}) %all-gather.6.cloned.1.call-update) | async-done | bytes 6553616 | tf_op jit(solution)/shard_map/all_gather | solution.py:60
  72.2 103.0 %all-gather.8.cloned.1.call-done = bf16[5120,896]{1,0:T(8,128)(2,1)} async-done(((bf16[160,896]{1,0:T(8,128)(2,1)}), bf16[5120,896]{1,0:T(8,128)(2,1)}) %all-gather.8.cloned.1.call-update) | async-done | bytes 9175056 | tf_op jit(solution)/shard_map/all_gather | solution.py:63
  175.2 12.7 %fusion.30 = f32[640,896]{1,0:T(8,128)} fusion(bf16[640,5120]{1,0:T(8,128)(2,1)} %all-gather.6.cloned.1.call-done, bf16[5120,896]{1,0:T(8,128)(2,1)} %all-gather.8.cloned.1.call-done), kind=kOutput, calls=%fused_computation.50 | convolution fusion | flops 5872025600 | bytes 18022400 | tf_op jit(solution)/shard_map/dot_general | solution.py:61
  187.9 89.2 %all-gather.10.cloned.1.call-done = bf16[896,5120]{0,1:T(8,128)(2,1)} async-done(((bf16[896,160]{0,1:T(8,128)(2,1)}), bf16[896,5120]{0,1:T(8,128)(2,1)}) %all-gather.10.cloned.1.call-update) | async-done | bytes 9175056 | tf_op jit(solution)/shard_map/all_gather | solution.py:69
  277.1 12.2 %convolution_convert_fusion = bf16[640,5120]{1,0:T(8,128)(2,1)} fusion(bf16[896,5120]{0,1:T(8,128)(2,1)} %all-gather.10.cloned.1.call-done, f32[640,896]{1,0:T(8,128)} %fusion.30), kind=kOutput, calls=%fused_computation.2 | convolution fusion | flops 5880463360 | bytes 18022400 | tf_op jit(solution)/shard_map/dot_general | solution.py:67
  289.9 44.7 %reduce-scatter.2.cloned.1.call-done = bf16[80,5120]{1,0:T(8,128)(2,1)} async-done(((bf16[640,5120]{1,0:T(8,128)(2,1)}), bf16[80,5120]{1,0:T(8,128)(2,1)}) %reduce-scatter.2.cloned.1.call-update) | async-done | bytes 819216 | tf_op jit(solution)/shard_map/reduce_scatter | solution.py:72
  334.6 1.5 fusion.16
  336.2 0.5 multiply_reduce_fusion
  336.7 0.6 copy-done.2
  337.3 0.6 fusion.13
  337.9 50.2 %all-gather.1 = f32[32,80,64]{1,2,0:T(8,128)S(1)} all-gather(f32[1,80,64]{1,2,0:T(8,128)S(1)} %fusion.19), channel_id=2, replica_groups=mesh['tm'=32,'tensor'=8] {'tm'}, dimensions={0}, use_global_device_ids=true | all-gather | bytes 675840 | tf_op jit(solution)/shard_map/all_gather | solution.py:10
  388.1 3.4 while.10
  388.2 0.1 copy.20
  388.3 0.1 copy.20
  388.4 0.1 copy.20
  388.6 0.1 copy.20
  388.7 0.1 copy.20
  388.9 0.1 copy.20
  389.0 0.1 copy.20
  389.2 0.1 copy.20
  389.3 0.1 copy.20
  389.4 0.1 copy.20
  389.6 0.1 copy.20
  389.7 0.1 copy.20
  391.6 0.6 add_bitcast_fusion
  (87 shorter events, 1.8 us)
Async XLA Ops:
  7.2 3.1 copy-start
  7.2 65.0 %all-gather.6.cloned.1.call-start = ((), (), s32[]{:S(2)}) async-start(), calls=%async_computation.1 | async-start | bytes 7372800 | tf_op jit(solution)/shard_map/all_gather | solution.py:60
  25.2 150.0 %all-gather.8.cloned.1.call-start = ((), (), s32[]{:S(2)}) async-start(), calls=%async_computation.2 | async-start | bytes 9461760 | tf_op jit(solution)/shard_map/all_gather | solution.py:63
  26.0 251.1 %all-gather.10.cloned.1.call-start = ((), (), s32[]{:S(2)}) async-start(), calls=%async_computation.3 | async-start | bytes 9461760 | tf_op jit(solution)/shard_map/all_gather | solution.py:69
  26.7 307.9 %reduce-scatter.2.cloned.1.call-start = ((), (), s32[]{:S(2)}) async-start(), calls=%async_computation.4 | async-start | bytes 7372800 | tf_op jit(solution)/shard_map/reduce_scatter | solution.py:72
  334.6 1.6 copy-start.1
  336.2 1.1 copy-start.2
  336.7 1.2 copy-start.3
  337.9 54.4 %copy-start.4 = (f32[80,64]{0,1:T(8,128)}, f32[80,64]{0,1:T(8,128)S(1)}, u32[]{:S(2)}) copy-start(f32[80,64]{0,1:T(8,128)S(1)} %fusion.13) | copy-start | bytes 61444
Sparse Core Ops, SparseCore 0:
  25.3 46.7 all-gather.5
  74.7 100.4 all-gather.7
  177.8 99.2 all-gather.9
  289.4 45.1 reduce-scatter.1
where the time goes:
time: 399 us
  waiting for transfers between devices  284 us (71%)
  blocking collectives  63.5 us (16%)
  matrix products  27.6 us (7%)
  between operations  15.2 us (4%)
  other arithmetic  4.66 us (1%)
    all_gather x1, waiting for transfers between devices, local(): lax.all_gather(up_weight, 'tm', axis=0, tiled=True)  103 us
    all_gather x1, waiting for transfers between devices, local(): lax.all_gather(down_weight, 'tm', axis=1, tiled=True)  89.2 us
    all_gather x1, blocking collectives, prefix(): gathered = lax.all_gather(part, axis)  50.2 us
    all_gather x1, waiting for transfers between devices, local(): normed = lax.all_gather(local_normed, 'tensor', axis=0, tiled=True)  45.4 us
    reduce_scatter x1, waiting for transfers between devices, local(): lax.psum_scatter(partial_sums.astype(jnp.bfloat16), 'tensor', scatter_dim...  44.7 us
    all_gather x1, blocking collectives, local(): modulation = lax.all_gather(piece_mod, 'tensor', axis=1, tiled=True)  13.3 us
    dot_general x1, matrix products, local(): jnp.dot(normed, lax.all_gather(up_weight, 'tm', axis=0, tiled=True), pref...  12.7 us
    dot_general x1, matrix products, local(): jnp.dot(activated, lax.all_gather(down_weight, 'tm', axis=1, tiled=True),...  12.2 us
  transfers between devices with their start and end apart: 4, of which 4 were waited for; matrix products, arithmetic and copies ran while one was open for 3% of the time, Pallas kernels for 0%

commit v1 on v0

--- a/solution.py
+++ b/solution.py
@@ -3,6 +3,7 @@
 import jax.numpy as jnp
 from jax import lax
 from jax.sharding import PartitionSpec as P
+from jax.lax import all_to_all, axis_size
 
 
 def prefix(part, axis, combine, identity):
@@ -57,7 +58,9 @@
         latent_bf, embed_weight, preferred_element_type=jnp.float32
     )
     local_normed = (normalize(hidden) * (1.0 + modulation[1]) + modulation[0]).astype(jnp.bfloat16)
-    normed = lax.all_gather(local_normed, "tensor", axis=0, tiled=True)
+    high = jnp.stack(tuple((local_normed for _ in range(axis_size("tensor")))), axis=0)
+    a_now = all_to_all(high, "tensor", split_axis=0, concat_axis=0)
+    normed = jnp.concatenate(a_now, axis=0)
     preact = jnp.dot(
         normed,
         lax.all_gather(up_weight, "tm", axis=0, tiled=True),

time: 399 us -> 338 us (0.85)
  waiting for transfers between devices: 284 us -> 143 us
  blocking collectives: 63.5 us -> 143 us
    all_gather x1, waiting for transfers between devices: 103 us -> 8.06 us  [local(): lax.all_gather(up_weight, 'tm', axis=0, tiled=True)]
    all_to_all x0 -> x1, blocking collectives: none -> 79.7 us  [local(): a_now = all_to_all(high, 'tensor', split_axis=0, concat_axis=0)]
    all_gather x1 -> x0, waiting for transfers between devices: 45.4 us -> none  [local(): normed = lax.all_gather(local_normed, 'tensor', axis=0, tiled=True)]
  transfers between devices with their start and end apart: 4 -> 3, of which waited for: 4 -> 3; matrix products, arithmetic and copies ran while one was open for 3% -> 5% of each run, Pallas kernels for 0% -> 0%
where the time goes in v1:
time: 338 us
  waiting for transfers between devices  143 us (42%)
  blocking collectives  143 us (42%)
  matrix products  27.4 us (8%)
  between operations  15.2 us (4%)
  other arithmetic  3.7 us (1%)
  local copies, waits for them, and re-layouts  3.6 us (1%)
    all_gather x1, waiting for transfers between devices, local(): lax.all_gather(down_weight, 'tm', axis=1, tiled=True)  89.2 us
    all_to_all x1, blocking collectives, local(): a_now = all_to_all(high, 'tensor', split_axis=0, concat_axis=0)  79.7 us
    all_gather x1, blocking collectives, prefix(): gathered = lax.all_gather(part, axis)  50.2 us
    reduce_scatter x1, waiting for transfers between devices, local(): lax.psum_scatter(partial_sums.astype(jnp.bfloat16), 'tensor', scatter_dim...  44.7 us
    all_gather x1, blocking collectives, local(): modulation = lax.all_gather(piece_mod, 'tensor', axis=1, tiled=True)  13.3 us
    dot_general x1, matrix products, local(): jnp.dot(normed, lax.all_gather(up_weight, 'tm', axis=0, tiled=True), pref...  12.7 us
    dot_general x1, matrix products, local(): jnp.dot(activated, lax.all_gather(down_weight, 'tm', axis=1, tiled=True),...  12.3 us
    all_gather x1, waiting for transfers between devices, local(): lax.all_gather(up_weight, 'tm', axis=0, tiled=True)  8.06 us
  transfers between devices with their start and end apart: 3, of which 3 were waited for; matrix products, arithmetic and copies ran while one was open for 5% of the time, Pallas kernels for 0%

profile of v1, /device:TPU:6, one launch (start us, length us, event | category | flops | bytes accessed | tf_op | source)
XLA Modules:
  0.0 337.7 jit_solution(7281761011453096863)
XLA Ops:
  7.2 0.7 all-gather.5.cloned.1.call-update
  8.0 0.7 all-gather.7.cloned.1.call-update
  9.5 0.2 fusion.29
  9.7 13.3 %all_gather.15 = f32[3,5120]{1,0:T(4,128)S(1)} all-gather(f32[3,640]{1,0:T(4,128)S(1)} %bitcast.48), channel_id=1, replica_groups=mesh['tm'=32,'tensor'=8] {'tensor'}, dimensions={1}, use_global_device_ids=true | all-gather | bytes 69120 | tf_op jit(solution)/shard_map/all_gather | solution.py:50
  23.0 1.6 fusion.28
  24.7 0.3 multiply_reduce_fusion.1
  25.1 0.3 add_convert_fusion
  25.4 0.8 stack.2
  26.2 79.7 %all_to_all.5 = bf16[8,80,5120]{2,1,0:T(8,128)(2,1)} all-to-all(bf16[8,80,5120]{2,1,0:T(8,128)(2,1)S(1)} %stack.2), channel_id=1, replica_groups=mesh['tm'=32,'tensor'=8] {'tensor'}, dimensions={0} | all-to-all | bytes 13107200 | tf_op jit(solution)/shard_map/all_to_all | solution.py:62
  105.9 8.1 %all-gather.5.cloned.1.call-done = bf16[5120,896]{1,0:T(8,128)(2,1)} async-done(((bf16[160,896]{1,0:T(8,128)(2,1)}), bf16[5120,896]{1,0:T(8,128)(2,1)}) %all-gather.5.cloned.1.call-update) | async-done | bytes 9175056 | tf_op jit(solution)/shard_map/all_gather | solution.py:66
  114.0 12.7 %fusion.30 = f32[640,896]{1,0:T(8,128)} fusion(bf16[640,5120]{1,0:T(8,128)(2,1)} %bitcast.41, bf16[5120,896]{1,0:T(8,128)(2,1)} %all-gather.5.cloned.1.call-done), kind=kOutput, calls=%fused_computation.50 | convolution fusion | flops 5872025600 | bytes 18022400 | tf_op jit(solution)/shard_map/dot_general | solution.py:64
  126.7 89.2 %all-gather.7.cloned.1.call-done = bf16[896,5120]{0,1:T(8,128)(2,1)} async-done(((bf16[896,160]{0,1:T(8,128)(2,1)}), bf16[896,5120]{0,1:T(8,128)(2,1)}) %all-gather.7.cloned.1.call-update) | async-done | bytes 9175056 | tf_op jit(solution)/shard_map/all_gather | solution.py:72
  215.9 12.3 %convolution_convert_fusion = bf16[640,5120]{1,0:T(8,128)(2,1)} fusion(bf16[896,5120]{0,1:T(8,128)(2,1)} %all-gather.7.cloned.1.call-done, f32[640,896]{1,0:T(8,128)} %fusion.30), kind=kOutput, calls=%fused_computation.2 | convolution fusion | flops 5880463360 | bytes 18022400 | tf_op jit(solution)/shard_map/dot_general | solution.py:70
  228.8 44.7 %reduce-scatter.2.cloned.1.call-done = bf16[80,5120]{1,0:T(8,128)(2,1)} async-done(((bf16[640,5120]{1,0:T(8,128)(2,1)}), bf16[80,5120]{1,0:T(8,128)(2,1)}) %reduce-scatter.2.cloned.1.call-update) | async-done | bytes 819216 | tf_op jit(solution)/shard_map/reduce_scatter | solution.py:75
  273.6 1.5 fusion.16
  275.1 0.5 multiply_reduce_fusion
  275.6 0.6 copy-done.3
  276.2 0.6 fusion.13
  276.8 50.2 %all-gather.1 = f32[32,80,64]{1,2,0:T(8,128)S(1)} all-gather(f32[1,80,64]{1,2,0:T(8,128)S(1)} %fusion.19), channel_id=2, replica_groups=mesh['tm'=32,'tensor'=8] {'tm'}, dimensions={0}, use_global_device_ids=true | all-gather | bytes 675840 | tf_op jit(solution)/shard_map/all_gather | solution.py:11
  327.0 3.4 %while.10 = (s32[]{:T(128)}, f32[80,64]{1,0:T(8,128)S(1)}, s32[]{:T(128)}, f32[32,80,64]{1,2,0:T(8,128)S(1)}, s32[]{:T(128)}, /*index=5*/s32[]{:T(128)}, s32[]{:T(128)}) while((s32[]{:T(128)}, f32[80,64]{1,0:T(8,128)S(1)}, s32[]{:T(128)}, f32[32,80,64]{1,2,0:T(8,128)S(1)}, s32[]{:T(128)}, /*index=5*/s32[]{:T(128)}, s32[]{:T(128)}) %tuple.28), condition=%wide.region_6.7_spmd, body=%wide.region_5.6_spmd.sunk | while | flops 5125 | bytes 143475 | solution.py:17
  327.1 0.1 copy.20
  327.2 0.1 copy.20
  327.4 0.1 copy.20
  327.5 0.1 copy.20
  327.7 0.1 copy.20
  327.8 0.1 copy.20
  327.9 0.1 copy.20
  328.1 0.1 copy.20
  328.2 0.1 copy.20
  328.4 0.1 copy.20
  328.5 0.1 copy.20
  330.5 0.6 add_bitcast_fusion
  (88 shorter events, 1.9 us)
Async XLA Ops:
  7.2 2.3 copy-start
  7.2 15.8 %copy-start.4 = (f32[1,80,64]{1,2,0:T(8,128)S(1)}, f32[1,80,64]{1,2,0:T(8,128)}, u32[]{:S(2)}) copy-start(f32[1,80,64]{1,2,0:T(8,128)} %param.11) | copy-start | bytes 61444
  7.2 15.8 %copy-start.2 = (bf16[64,5120]{1,0:T(8,128)(2,1)S(1)}, bf16[64,5120]{1,0:T(8,128)(2,1)}, u32[]{:S(2)}) copy-start(bf16[64,5120]{1,0:T(8,128)(2,1)} %param.15) | copy-start | bytes 1966084
  7.2 106.8 %all-gather.5.cloned.1.call-start = ((), (), s32[]{:S(2)}) async-start(), calls=%async_computation.2 | async-start | bytes 9461760 | tf_op jit(solution)/shard_map/all_gather | solution.py:66
  7.9 207.9 %all-gather.7.cloned.1.call-start = ((), (), s32[]{:S(2)}) async-start(), calls=%async_computation.3 | async-start | bytes 9461760 | tf_op jit(solution)/shard_map/all_gather | solution.py:72
  8.7 264.9 %reduce-scatter.2.cloned.1.call-start = ((), (), s32[]{:S(2)}) async-start(), calls=%async_computation.4 | async-start | bytes 7372800 | tf_op jit(solution)/shard_map/reduce_scatter | solution.py:75
  273.6 1.6 copy-start.1
  275.1 1.1 copy-start.3
  276.8 54.4 %copy-start.5 = (f32[80,64]{0,1:T(8,128)}, f32[80,64]{0,1:T(8,128)S(1)}, u32[]{:S(2)}) copy-start(f32[80,64]{0,1:T(8,128)S(1)} %fusion.13) | copy-start | bytes 61444
Sparse Core Ops, SparseCore 0:
  10.6 103.3 all-gather.4
  116.5 99.2 all-gather.6
  228.3 45.2 reduce-scatter.1
